TPU v7x, 256 devices: a whole 4x4x8 slice. The times are simulated.
256 devices in a mesh: gossip: 16 (over z, x_lo), fsdp: 16 (over x_hi, y, core).
Axes of the slice: x: 4 (x_hi: 2, x_lo: 2; x = x_hi * 2 + x_lo), y: 4, z: 8, core: 2. Of those that a mesh axis runs over, the one named last changes fastest.
Arguments:
- inputs: bfloat16 [16, 2048, 2048], P('gossip', 'fsdp'), may hold values from -6 to 6
- out_grad: bfloat16 [16, 2048, 2048], P('gossip', 'fsdp'), may hold values from -6 to 6
- norm_gain: float32 [16, 2048], P('gossip'), may hold values from 0.5 to 1.5
- w_qkv: bfloat16 [16, 16, 2048, 384], P('gossip', 'fsdp'), may hold values from -64 to 64
- w_out: bfloat16 [16, 16, 128, 2048], P('gossip', 'fsdp'), may hold values from -6 to 6
- mom_qkv: bfloat16 [16, 16, 2048, 384], P('gossip', 'fsdp'), may hold values from -6 to 6
- mom_out: bfloat16 [16, 16, 128, 2048], P('gossip', 'fsdp'), may hold values from -6 to 6
- step_index: int32 [1], replicated, may hold values from 0 to 11
Outputs:
- new_qkv: bfloat16 [16, 16, 2048, 384], P('gossip', 'fsdp')
- new_out: bfloat16 [16, 16, 128, 2048], P('gossip', 'fsdp')
- new_mom_qkv: bfloat16 [16, 16, 2048, 384], P('gossip', 'fsdp')
- new_mom_out: bfloat16 [16, 16, 128, 2048], P('gossip', 'fsdp')
All inputs are finite; a program needn't handle non-finite values.
Results may differ from a plain program's by a relative error of at most 0.0085.
Values may be sent and summed in bfloat16 or wider, within the bound.
A program may use at most 128 MiB of HBM per device.

v0:
```python
from functools import partial
import math
import jax
import jax.numpy as jnp
from jax import lax
from jax.sharding import PartitionSpec as P

HEADS = 16
LEVELS = 3
BETA = 0.9
RATE = 0.1
EPSILON = 1e-05


def for_sending(value):
    return jax.tree.map(lambda a: a.astype(jnp.bfloat16) if a.dtype == jnp.float32 else a, value)


def shifted(value, axis, by):
    size = lax.axis_size(axis)
    return lax.ppermute(value, axis, [(i, (i + by) % size) for i in range(size)])


def rotate(tensor, positions):
    half_width = tensor.shape[-1] // 2
    frequency = jnp.exp(
        -math.log(10000.0) * 2.0 * jnp.arange(half_width, dtype=jnp.float32) / tensor.shape[-1]
    )
    angles = positions.astype(jnp.float32)[:, None] * frequency[None, :]
    cosine = jnp.cos(angles)
    sine_vals = jnp.sin(angles)
    first = tensor[..., :half_width]
    second = tensor[..., half_width:]
    return jnp.concatenate(
        [first * cosine - second * sine_vals, second * cosine + first * sine_vals], -1
    )


def unrotate(grad_in, positions):
    half_width = grad_in.shape[-1] // 2
    frequency = jnp.exp(
        -math.log(10000.0) * 2.0 * jnp.arange(half_width, dtype=jnp.float32) / grad_in.shape[-1]
    )
    angles = positions.astype(jnp.float32)[:, None] * frequency[None, :]
    cosine = jnp.cos(angles)
    sine_vals = jnp.sin(angles)
    first = grad_in[..., :half_width]
    second = grad_in[..., half_width:]
    return jnp.concatenate(
        [first * cosine + second * sine_vals, second * cosine - first * sine_vals], -1
    )


def attend(queries, key_rows, val_rows):
    seq_len, head_dim = queries.shape
    block_len = min(512, seq_len)
    scale = 1.0 / math.sqrt(head_dim)
    outputs = []
    prob_list = []
    for block_num in range(seq_len // block_len):
        begin = block_num * block_len
        key_end = begin + block_len
        scores = (
            jnp.dot(
                queries[begin:key_end], key_rows[:key_end].T, preferred_element_type=jnp.float32
            )
            * scale
        )
        row_pos = begin + jnp.arange(block_len)[:, None]
        col_pos = jnp.arange(key_end)[None, :]
        scores = jnp.where(col_pos <= row_pos, scores, -jnp.inf)
        top = jnp.max(scores, -1, keepdims=True)
        weights = jnp.exp(scores - top)
        weights = weights / jnp.sum(weights, -1, keepdims=True)
        prob_list.append(weights)
        outputs.append(
            jnp.dot(
                weights.astype(jnp.bfloat16), val_rows[:key_end], preferred_element_type=jnp.float32
            )
        )
    return (jnp.concatenate(outputs, 0).astype(jnp.bfloat16), prob_list)


def attend_back(queries, key_rows, val_rows, prob_list, grad_att):
    seq_len, head_dim = queries.shape
    block_len = min(512, seq_len)
    scale = 1.0 / math.sqrt(head_dim)
    grad_q_list = []
    grad_keys = jnp.zeros((seq_len, head_dim), jnp.float32)
    grad_vals = jnp.zeros((seq_len, head_dim), jnp.float32)
    for block_num in range(seq_len // block_len):
        begin = block_num * block_len
        key_end = begin + block_len
        weights = prob_list[block_num]
        weights_b = weights.astype(jnp.bfloat16)
        grad_block = grad_att[begin:key_end]
        grad_probs = jnp.dot(grad_block, val_rows[:key_end].T, preferred_element_type=jnp.float32)
        centred = grad_probs - jnp.sum(weights * grad_probs, -1, keepdims=True)
        grad_scores = (weights * centred * scale).astype(jnp.bfloat16)
        grad_q_list.append(
            jnp.dot(grad_scores, key_rows[:key_end], preferred_element_type=jnp.float32)
        )
        grad_keys = grad_keys.at[:key_end].add(
            jnp.dot(grad_scores.T, queries[begin:key_end], preferred_element_type=jnp.float32)
        )
        grad_vals = grad_vals.at[:key_end].add(
            jnp.dot(weights_b.T, grad_block, preferred_element_type=jnp.float32)
        )
    return (jnp.concatenate(grad_q_list, 0), grad_keys, grad_vals)


def advance(weight, moment, gradient, rate):
    moved_m = (BETA * moment.astype(jnp.float32) + gradient.astype(jnp.float32)).astype(
        jnp.bfloat16
    )
    moved_w = (weight.astype(jnp.float32) - rate * moved_m.astype(jnp.float32)).astype(jnp.bfloat16)
    return (moved_w, moved_m)


def send_updated(payload, by):
    return jax.tree.map(
        lambda part, own: part.astype(own.dtype),
        shifted(for_sending(payload), "gossip", by),
        payload,
    )


def to_partner(mover, payload, step_index):
    branches = [partial(mover, by=1 << bit_level) for bit_level in range(LEVELS)]
    exponent = jnp.remainder(step_index[0], LEVELS)
    return lax.switch(exponent, branches, payload)


def average(own, other):
    return ((own.astype(jnp.float32) + other.astype(jnp.float32)) * 0.5).astype(jnp.bfloat16)


def per_device(inputs, out_grad, norm_gain, w_qkv, w_out, mom_qkv, mom_out, step_index):
    rate = RATE * (step_index[0].astype(jnp.float32) + 1.0) / (4.0 * LEVELS)
    rows_f = inputs[0].astype(jnp.float32)
    stats = lax.rsqrt(jnp.mean(rows_f * rows_f, -1, keepdims=True) + EPSILON)
    normed = (rows_f * stats * norm_gain[0][None, :]).astype(jnp.bfloat16)
    all_normed = lax.all_gather(normed, "fsdp", axis=0, tiled=True)
    seq_len, width = all_normed.shape
    head_qkv = w_qkv[0]
    head_out = w_out[0]
    head_count, head_dim = (head_out.shape[0], head_out.shape[1])
    positions = jnp.arange(seq_len)
    out_scale = 1.0 / math.sqrt(HEADS * head_dim)
    projected = jnp.einsum(
        "td,hde->hte", all_normed, head_qkv, preferred_element_type=jnp.float32
    ) * (1.0 / math.sqrt(width))
    queries = rotate(projected[..., :head_dim], positions).astype(jnp.bfloat16)
    key_rows = rotate(projected[..., head_dim : 2 * head_dim], positions).astype(jnp.bfloat16)
    val_rows = projected[..., 2 * head_dim :].astype(jnp.bfloat16)
    attended, prob_list = jax.vmap(attend)(queries, key_rows, val_rows)
    piece = lax.all_gather(out_grad[0], "fsdp", axis=0, tiled=True)
    out_sum = jnp.zeros((head_count, head_dim, width), jnp.float32)
    count = piece.shape[0]
    att_rows = lax.slice_in_dim(attended, 0, count, axis=1)
    out_sum = out_sum + jnp.einsum(
        "hte,td->hed", att_rows, piece, preferred_element_type=jnp.float32
    )
    new_rows = (
        jnp.einsum("td,hed->hte", piece, head_out, preferred_element_type=jnp.float32) * out_scale
    ).astype(jnp.bfloat16)
    grad_att = new_rows
    out_sum, grad_att = (out_sum, grad_att)
    grad_out = (out_sum * out_scale).astype(jnp.bfloat16)
    grad_q, grad_k, grad_v = jax.vmap(attend_back)(queries, key_rows, val_rows, prob_list, grad_att)
    grad_proj = jnp.concatenate(
        [unrotate(grad_q, positions), unrotate(grad_k, positions), grad_v], -1
    )
    grad_proj = (grad_proj * (1.0 / math.sqrt(width))).astype(jnp.bfloat16)
    grad_qkv = jnp.einsum(
        "td,hte->hde", all_normed, grad_proj, preferred_element_type=jnp.float32
    ).astype(jnp.bfloat16)[None]
    grad_out = grad_out[None]
    moved_qkv, moved_mqkv = advance(w_qkv, mom_qkv, grad_qkv, rate)
    moved_out, moved_mout = advance(w_out, mom_out, grad_out, rate)
    other_qkv, other_out, other_mqkv, other_mout = to_partner(
        send_updated, (moved_qkv, moved_out, moved_mqkv, moved_mout), step_index
    )
    return (
        average(moved_qkv, other_qkv),
        average(moved_out, other_out),
        average(moved_mqkv, other_mqkv),
        average(moved_mout, other_mout),
    )


def solution(mesh):
    return jax.shard_map(
        per_device,
        mesh=mesh,
        in_specs=(
            P("gossip", "fsdp", None),
            P("gossip", "fsdp", None),
            P("gossip", None),
            P("gossip", "fsdp", None, None),
            P("gossip", "fsdp", None, None),
            P("gossip", "fsdp", None, None),
            P("gossip", "fsdp", None, None),
            P(),
        ),
        out_specs=(
            P("gossip", "fsdp", None, None),
            P("gossip", "fsdp", None, None),
            P("gossip", "fsdp", None, None),
            P("gossip", "fsdp", None, None),
        ),
        check_vma=False,
    )
```

profile of v0, /device:TPU:1, one launch (start us, length us, event | category | flops | bytes accessed | tf_op | source)
XLA Modules:
  0.0 339.4 jit_solution(3943303239801922108)
XLA Ops:
  8.6 2.0 fusion.65
  12.1 1.6 copy.12
  13.7 1.6 copy.13
  15.4 77.8 %all-gather.4.cloned.1.call-done = bf16[2048,2048]{1,0:T(8,128)(2,1)} async-done(((bf16[128,2048]{1,0:T(8,128)(2,1)}), bf16[2048,2048]{1,0:T(8,128)(2,1)}) %all-gather.4.cloned.1.call-update) | async-done | bytes 8388624 | tf_op jit(solution)/shard_map/all_gather | solution.py:143
  93.2 5.9 %fusion.158 = (bf16[1,2048,384]{1,2,0:T(8,128)(2,1)S(1)}, f32[1,2048,384]{1,2,0:T(8,128)S(1)}) fusion(bf16[2048,2048]{1,0:T(8,128)(2,1)} %all-gather.4.cloned.1.call-done, bf16[1,1,2048,384]{3,2,1,0:T(8,128)(2,1)S(1)} %copy-done.5), kind=kOutput, calls=%fused_computation.199 | convolution fusion | flops 3222798336 | bytes 14680064 | tf_op jit(solution)/shard_map/td,hde->hte/dot_general | solution.py:150
  99.1 2.6 fusion.93
  102.7 68.8 %all-gather.6.cloned.1.call-done = bf16[1,2048,2048]{2,1,0:T(8,128)(2,1)} async-done(((bf16[1,128,2048]{2,1,0:T(8,128)(2,1)}), bf16[1,2048,2048]{2,1,0:T(8,128)(2,1)}) %all-gather.6.cloned.1.call-update) | async-done | bytes 8388624 | tf_op jit(solution)/shard_map/all_gather | solution.py:157
  171.6 6.3 %fusion.35 = bf16[1,2048,128]{1,2,0:T(8,128)(2,1)S(1)} fusion(bf16[1,2048,2048]{2,1,0:T(8,128)(2,1)} %all-gather.6.cloned.1.call-done, bf16[1,1,128,2048]{3,2,1,0:T(8,128)(2,1)S(1)} %copy-done.1), kind=kOutput, calls=%fused_computation.48 | convolution fusion | flops 1074266112 | bytes 9437184 | tf_op jit(solution)/shard_map/td,hed->hte/dot_general | solution.py:165
  198.3 2.1 fusion.98
  200.4 2.1 fusion.101
  202.5 2.1 fusion.104
  204.6 2.2 fusion.107
  210.0 3.8 %fusion.8 = (bf16[1,1,2048,384]{2,3,1,0:T(8,128)(2,1)S(1)}, bf16[1,1,2048,384]{2,3,1,0:T(8,128)(2,1)S(1)}) fusion(bf16[1,1,2048,384]{2,3,1,0:T(8,128)(2,1)S(1)} %copy-done.6, f32[]{:T(128)} %bitcast, bf16[2048,2048]{1,0:T(8,128)(2,1)S(1)} %bitcast.244, f32[2048,384]{0,1:T(8,128)S(1)} %fusion.22, bf16[1,1,2048,384]{2,3,1,0:T(8,128)(2,1)S(1)} %copy-done.7), kind=kOutput, calls=%fused_computation.16 | convolution fusion | flops 3231449088 | bytes 17825796 | tf_op jit(solution)/shard_map/td,hte->hde/dot_general | solution.py:175
  213.8 2.4 fusion.60
  216.2 102.7 %conditional.3 = (f32[1,1,128,2048]{3,2,1,0:T(8,128)}, f32[1,1,128,2048]{3,2,1,0:T(8,128)}, f32[1,1,2048,384]{2,3,1,0:T(8,128)}, f32[1,1,2048,384]{2,3,1,0:T(8,128)}) conditional(s32[]{:T(128)} %clamp.3, (bf16[1,1,2048,384]{2,3,1,0:T(8,128)(2,1)S(1)}, bf16[1,1,128,2048]{3,2,1,0:T(8,128)(2,1)}, ...), branch_computations={%region_13.14_spmd, %region_14.15_spmd, %region_15.16_spmd} | conditional | flops 524288 | bytes 35651776
  223.2 2.5 collective-permute-start.7
  225.7 74.8 %collective-permute-done.5 = bf16[1,1,128,2048]{3,2,1,0:T(8,128)(2,1)S(1)} collective-permute-done((bf16[1,1,128,2048]{3,2,1,0:T(8,128)(2,1)}, bf16[1,1,128,2048]{3,2,1,0:T(8,128)(2,1)S(1)}, u32[]{:S(2)}, u32[]{:S(2)}) %collective-permute-start.5) | collective-permute-done | bytes 524320 | tf_op jit(solution)/shard_map/cond/branch_1_fun/ppermute | solution.py:21
  301.6 10.1 %collective-permute-done.7 = bf16[1,1,128,2048]{3,2,1,0:T(8,128)(2,1)S(1)} collective-permute-done((bf16[1,1,128,2048]{3,2,1,0:T(8,128)(2,1)}, bf16[1,1,128,2048]{3,2,1,0:T(8,128)(2,1)S(1)}, u32[]{:S(2)}, u32[]{:S(2)}) %collective-permute-start.7) | collective-permute-done | bytes 524320 | tf_op jit(solution)/shard_map/cond/branch_1_fun/ppermute | solution.py:21
  312.8 3.1 copy.33
  315.9 3.1 copy.36
  318.9 2.3 fusion.62
  321.2 3.5 %fusion.10 = bf16[1,1,2048,384]{2,3,1,0:T(8,128)(2,1)} fusion(f32[1,1,2048,384]{2,3,1,0:T(8,128)} %get-tuple-element.205, bf16[1,1,2048,384]{2,3,1,0:T(8,128)(2,1)S(1)} %get-tuple-element.229), kind=kLoop, calls=%fused_computation.18 | loop fusion | flops 3145728 | bytes 6291456 | tf_op jit(solution)/shard_map/convert_element_type | solution.py:135
  324.7 2.7 copy.27
  328.4 2.4 multiply_convert_fusion.1
  (90 shorter events, 38.3 us)
Async XLA Ops:
  7.2 4.9 %copy-start.5 = (bf16[1,1,2048,384]{3,2,1,0:T(8,128)(2,1)S(1)}, bf16[1,1,2048,384]{3,2,1,0:T(8,128)(2,1)}, u32[]{:S(2)}) copy-start(bf16[1,1,2048,384]{3,2,1,0:T(8,128)(2,1)} %param.34) | copy-start | bytes 4718596
  7.2 6.6 %copy-start.4 = (bf16[1,1,2048,384]{3,2,1,0:T(8,128)(2,1)S(1)}, bf16[1,1,2048,384]{3,2,1,0:T(8,128)(2,1)}, u32[]{:S(2)}) copy-start(bf16[1,1,2048,384]{3,2,1,0:T(8,128)(2,1)} %param.36) | copy-start | bytes 4718596
  7.2 86.1 %all-gather.4.cloned.1.call-start = ((), (), s32[]{:S(2)}) async-start(), calls=%async_computation | async-start | bytes 8912896 | tf_op jit(solution)/shard_map/all_gather | solution.py:143
  10.7 160.9 %all-gather.6.cloned.1.call-start = ((), (), s32[]{:S(2)}) async-start(), calls=%async_computation.1 | async-start | bytes 8912896 | tf_op jit(solution)/shard_map/all_gather | solution.py:157
  99.1 3.2 copy-start.9
  102.1 69.4 %copy-start.1 = (bf16[1,1,128,2048]{3,2,1,0:T(8,128)(2,1)S(1)}, bf16[1,1,128,2048]{3,2,1,0:T(8,128)(2,1)}, u32[]{:S(2)}) copy-start(bf16[1,1,128,2048]{3,2,1,0:T(8,128)(2,1)} %param.35) | copy-start | bytes 1572868
  177.9 1.4 copy-start.10
  198.3 9.6 %slice-start.2 = ((s8[8388608]{0:T(1024)(128)(4,1)}), s8[4194304]{0:T(1024)(128)(4,1)S(1)}, s32[]{:S(2)}) async-start(s8[8388608]{0:T(1024)(128)(4,1)} %bitcast.243), calls=%async_computation.4 | async-start | bytes 8388608
  206.8 1.4 copy-start.6
  206.8 1.9 copy-start.7
  206.8 3.1 slice-start.3
  206.8 6.9 %slice-start = ((s8[8388608]{0:T(1024)(128)(4,1)}), s8[4194304]{0:T(1024)(128)(4,1)S(1)}, s32[]{:S(2)}) async-start(s8[8388608]{0:T(1024)(128)(4,1)} %bitcast.236), calls=%async_computation.2 | async-start | bytes 8388608
  210.0 3.8 %slice-start.1 = ((s8[8388608]{0:T(1024)(128)(4,1)}), s8[4194304]{0:T(1024)(128)(4,1)S(1)}, s32[]{:S(2)}) async-start(s8[8388608]{0:T(1024)(128)(4,1)} %bitcast.236), calls=%async_computation.3 | async-start | bytes 8388608
  210.0 3.8 %copy-start.2 = (bf16[1,1,128,2048]{3,2,1,0:T(8,128)(2,1)S(1)}, bf16[1,1,128,2048]{3,2,1,0:T(8,128)(2,1)}, u32[]{:S(2)}) copy-start(bf16[1,1,128,2048]{3,2,1,0:T(8,128)(2,1)} %param.35) | copy-start | bytes 1572868
  210.0 3.8 %copy-start.8 = (bf16[1,1,128,2048]{3,2,1,0:T(8,128)(2,1)S(1)}, bf16[1,1,128,2048]{3,2,1,0:T(8,128)(2,1)}, u32[]{:S(2)}) copy-start(bf16[1,1,128,2048]{3,2,1,0:T(8,128)(2,1)} %param.37) | copy-start | bytes 1572868
  217.8 95.0 %collective-permute-start.4 = (bf16[1,1,2048,384]{3,2,1,0:T(8,128)(2,1)}, bf16[1,1,2048,384]{3,2,1,0:T(8,128)(2,1)}, u32[]{:S(2)}, u32[]{:S(2)}) collective-permute-start(bf16[1,1,2048,384]{3,2,1,0:T(8,128)(2,1)} %copy.20), channel_id=1, source_target_pairs={{0,32},{16,48},{32,64},{48,80},{64,96},{80,112},{96,128},{112,144}... | collective-permute-start | bytes 4718600 | tf_op jit(solution)/shard_map/cond/branch_1_fun/ppermute | solution.py:21
  220.6 95.2 %collective-permute-start.6 = (bf16[1,1,2048,384]{3,2,1,0:T(8,128)(2,1)}, bf16[1,1,2048,384]{3,2,1,0:T(8,128)(2,1)}, u32[]{:S(2)}, u32[]{:S(2)}) collective-permute-start(bf16[1,1,2048,384]{3,2,1,0:T(8,128)(2,1)} %copy.21), channel_id=1, source_target_pairs={{0,32},{16,48},{32,64},{48,80},{64,96},{80,112},{96,128},{112,144}... | collective-permute-start | bytes 4718600 | tf_op jit(solution)/shard_map/cond/branch_1_fun/ppermute | solution.py:21
  221.9 78.6 %collective-permute-start.5 = (bf16[1,1,128,2048]{3,2,1,0:T(8,128)(2,1)}, bf16[1,1,128,2048]{3,2,1,0:T(8,128)(2,1)S(1)}, u32[]{:S(2)}, u32[]{:S(2)}) collective-permute-start(bf16[1,1,128,2048]{3,2,1,0:T(8,128)(2,1)} %get-tuple-element.165), channel_id=1, source_target_pairs={{0,32},{16,48},{32,64},{48,80},{64,96},{80,112},{96,128},{112,144}... | collective-permute-start | bytes 1572872 | tf_op jit(solution)/shard_map/cond/branch_1_fun/ppermute | solution.py:21
  223.2 88.5 %collective-permute-start.7 = (bf16[1,1,128,2048]{3,2,1,0:T(8,128)(2,1)}, bf16[1,1,128,2048]{3,2,1,0:T(8,128)(2,1)S(1)}, u32[]{:S(2)}, u32[]{:S(2)}) collective-permute-start(bf16[1,1,128,2048]{3,2,1,0:T(8,128)(2,1)} %get-tuple-element.167), channel_id=1, source_target_pairs={{0,32},{16,48},{32,64},{48,80},{64,96},{80,112},{96,128},{112,144}... | collective-permute-start | bytes 1572872 | tf_op jit(solution)/shard_map/cond/branch_1_fun/ppermute | solution.py:21
  324.7 2.7 copy-start
  324.7 2.7 copy-start.3
Sparse Core Ops, SparseCore 0:
  11.3 81.8 all-gather.3
  96.0 75.5 all-gather.5
where the time goes:
time: 343 us; the launch traced here: 339 us
  waiting for transfers between devices  232 us (68%)
  matrix products  33.6 us (10%)
  other arithmetic  31.2 us (9%)
  local copies, waits for them, and re-layouts  20.5 us (6%)
  between operations  15.3 us (4%)
  starting transfers between devices  6.38 us (2%)
    ppermute x4, waiting for transfers between devices, shifted(): lax.ppermute(value, axis, [(i, (i + by) % size) for i in range(size)])  84.9 us
    all_gather x1, waiting for transfers between devices, per_device(): all_normed = lax.all_gather(normed, 'fsdp', axis=0, tiled=True)  77.8 us
    all_gather x1, waiting for transfers between devices, per_device(): piece = lax.all_gather(out_grad[0], 'fsdp', axis=0, tiled=True)  68.8 us
    unnamed x34, local copies, waits for them, and re-layouts  10.7 us
    another operation x4, local copies, waits for them, and re-layouts  9.23 us
    convert_element_type x4, other arithmetic, average(): ((own.astype(jnp.float32) + other.astype(jnp.float32)) * 0.5).astype(jnp....  9.15 us
    unnamed x6, other arithmetic  8.45 us
  transfers between devices with their start and end apart: 6, of which 4 were waited for; matrix products, arithmetic and copies ran while one was open for 6% of the time, Pallas kernels for 0%

commit v1 on v0

--- a/solution.py
+++ b/solution.py
@@ -154,7 +154,9 @@
     key_rows = rotate(projected[..., head_dim : 2 * head_dim], positions).astype(jnp.bfloat16)
     val_rows = projected[..., 2 * head_dim :].astype(jnp.bfloat16)
     attended, prob_list = jax.vmap(attend)(queries, key_rows, val_rows)
-    piece = lax.all_gather(out_grad[0], "fsdp", axis=0, tiled=True)
+    piece = jnp.concatenate(
+        lax.all_to_all(jnp.stack([out_grad[0]] * lax.axis_size("fsdp")), "fsdp", 0, 0), axis=0
+    )
     out_sum = jnp.zeros((head_count, head_dim, width), jnp.float32)
     count = piece.shape[0]
     att_rows = lax.slice_in_dim(attended, 0, count, axis=1)

time: 343 us -> 359 us (1.047)
  starting transfers between devices: 6.38 us -> 15.5 us
  matrix products: 33.6 us -> 37.5 us
    all_to_all x0 -> x1, waiting for transfers between devices: none -> 126 us  [per_device(): lax.all_to_all(jnp.stack([out_grad[0]] * lax.axis_size('fsdp')), 'fsdp',...]
    all_gather x1 -> x0, waiting for transfers between devices: 68.8 us -> none  [per_device(): piece = lax.all_gather(out_grad[0], 'fsdp', axis=0, tiled=True)]
    all_gather x1, waiting for transfers between devices: 77.8 us -> 17.5 us  [per_device(): all_normed = lax.all_gather(normed, 'fsdp', axis=0, tiled=True)]
    all_to_all x0 -> x1, starting transfers between devices: none -> 8.44 us  [per_device(): lax.all_to_all(jnp.stack([out_grad[0]] * lax.axis_size('fsdp')), 'fsdp',...]
    another operation x4 -> x5, local copies, waits for them, and re-layouts: 9.23 us -> 14.6 us
    dot_general x1, matrix products: 2.42 us -> 6.12 us  [per_device(): jnp.einsum('hte,td->hed', att_rows, piece, preferred_element_type=jnp.flo...]
    unnamed x34 -> x24, local copies, waits for them, and re-layouts: 10.7 us -> 8.57 us
    unnamed x6 -> x5, other arithmetic: 8.45 us -> 8.45 us
where the time goes in v1:
time: 359 us; the launch traced here: 353 us
  waiting for transfers between devices  230 us (64%)
  matrix products  37.5 us (10%)
  other arithmetic  31.2 us (9%)
  local copies, waits for them, and re-layouts  23.4 us (7%)
  between operations  15.8 us (4%)
  starting transfers between devices  15.5 us (4%)
    all_to_all x1, waiting for transfers between devices, per_device(): lax.all_to_all(jnp.stack([out_grad[0]] * lax.axis_size('fsdp')), 'fsdp',...  126 us
    ppermute x4, waiting for transfers between devices, shifted(): lax.ppermute(value, axis, [(i, (i + by) % size) for i in range(size)])  85.5 us
    all_gather x1, waiting for transfers between devices, per_device(): all_normed = lax.all_gather(normed, 'fsdp', axis=0, tiled=True)  17.5 us
    another operation x4, local copies, waits for them, and re-layouts  9.27 us
    convert_element_type x4, other arithmetic, average(): ((own.astype(jnp.float32) + other.astype(jnp.float32)) * 0.5).astype(jnp....  9.15 us
    unnamed x24, local copies, waits for them, and re-layouts  8.57 us
    unnamed x5, other arithmetic  8.45 us
    all_to_all x1, starting transfers between devices, per_device(): lax.all_to_all(jnp.stack([out_grad[0]] * lax.axis_size('fsdp')), 'fsdp',...  8.44 us
  transfers between devices with their start and end apart: 6, of which 4 were waited for; matrix products, arithmetic and copies ran while one was open for 6% of the time, Pallas kernels for 0%

profile of v1, /device:TPU:1, one launch (start us, length us, event | category | flops | bytes accessed | tf_op | source)
XLA Modules:
  0.0 352.8 jit_solution(5419188947566011367)
XLA Ops:
  10.5 5.3 %stack.3 = bf16[16,128,2048]{2,1,0:T(8,128)(2,1)} broadcast(bf16[128,2048]{1,0:T(8,128)(2,1)} %bitcast.219), dimensions={1,2} | broadcast | bytes 8912896 | tf_op jit(solution)/shard_map/stack | solution.py:158
  15.8 8.4 %all-to-all-start = ((bf16[16,128,2048]{2,1,0:T(8,128)(2,1)}), bf16[16,128,2048]{2,1,0:T(8,128)(2,1)}, u32[]{:S(2)}, u32[]{:S(2)}) async-start(bf16[16,128,2048]{2,1,0:T(8,128)(2,1)} %stack.3), calls=%async_computation | async-start | bytes 16777216 | tf_op jit(solution)/shard_map/all_to_all | solution.py:158
  25.1 2.6 copy.12
  29.4 126.5 %all-to-all-done = bf16[16,128,2048]{2,1,0:T(8,128)(2,1)} async-done(((bf16[16,128,2048]{2,1,0:T(8,128)(2,1)}), bf16[16,128,2048]{2,1,0:T(8,128)(2,1)}, u32[]{:S(2)}, u32[]{:S(2)}) %all-to-all-start) | async-done | bytes 8388640 | tf_op jit(solution)/shard_map/all_to_all | solution.py:158
  155.9 6.4 %fusion.25 = bf16[1,2048,128]{1,2,0:T(8,128)(2,1)S(1)} fusion(bf16[2048,2048]{1,0:T(8,128)(2,1)} %bitcast.14, bf16[1,1,128,2048]{3,2,1,0:T(8,128)(2,1)S(1)} %copy-done.1), kind=kOutput, calls=%fused_computation.48 | convolution fusion | flops 1074266112 | bytes 9437184 | tf_op jit(solution)/shard_map/td,hed->hte/dot_general | solution.py:167
  162.3 17.5 %all-gather.2.cloned.1.call-done = bf16[2048,2048]{1,0:T(8,128)(2,1)} async-done(((bf16[128,2048]{1,0:T(8,128)(2,1)}), bf16[2048,2048]{1,0:T(8,128)(2,1)}) %all-gather.2.cloned.1.call-update) | async-done | bytes 8388624 | tf_op jit(solution)/shard_map/all_gather | solution.py:143
  179.8 5.9 %fusion.134 = (bf16[1,2048,384]{1,2,0:T(8,128)(2,1)S(1)}, f32[1,2048,384]{1,2,0:T(8,128)S(1)}) fusion(bf16[2048,2048]{1,0:T(8,128)(2,1)} %all-gather.2.cloned.1.call-done, bf16[1,1,2048,384]{3,2,1,0:T(8,128)(2,1)S(1)} %copy-done.4), kind=kOutput, calls=%fused_computation.195 | convolution fusion | flops 3222798336 | bytes 14680064 | tf_op jit(solution)/shard_map/td,hde->hte/dot_general | solution.py:150
  185.7 2.6 fusion.69
  208.7 2.1 fusion.74
  210.8 2.1 fusion.77
  212.9 2.1 fusion.80
  214.9 2.2 fusion.83
  218.3 6.1 %fusion.36 = (bf16[1,1,128,2048]{3,2,1,0:T(8,128)(2,1)}, bf16[1,1,128,2048]{3,2,1,0:T(8,128)(2,1)}) fusion(bf16[1,1,128,2048]{3,2,1,0:T(8,128)(2,1)S(1)} %copy-done.1, f32[]{:T(128)} %bitcast, bf16[2048,2048]{1,0:T(8,128)(2,1)} %bitcast.14, bf16[512,128]{1,0:T(8,128)(2,1)S(1)} %convolution_convert_fusion.1, ...), kind=kOutput, calls=%fused_computation.81 | convolution fusion | flops 1078984704 | bytes 11010052 | tf_op jit(solution)/shard_map/hte,td->hed/dot_general | solution.py:163
  224.4 3.9 %fusion.4 = (bf16[1,1,2048,384]{2,3,1,0:T(8,128)(2,1)S(1)}, bf16[1,1,2048,384]{2,3,1,0:T(8,128)(2,1)S(1)}) fusion(bf16[1,1,2048,384]{2,3,1,0:T(8,128)(2,1)S(1)} %copy-done.5, f32[]{:T(128)} %bitcast, bf16[2048,2048]{1,0:T(8,128)(2,1)S(1)} %bitcast.222, f32[2048,384]{0,1:T(8,128)S(1)} %fusion.18, bf16[1,1,2048,384]{2,3,1,0:T(8,128)(2,1)S(1)} %copy-done.6), kind=kOutput, calls=%fused_computation.12 | convolution fusion | flops 3231449088 | bytes 17825796 | tf_op jit(solution)/shard_map/td,hte->hde/dot_general | solution.py:177
  228.3 104.1 %conditional.3 = (f32[1,1,128,2048]{3,2,1,0:T(8,128)}, f32[1,1,128,2048]{3,2,1,0:T(8,128)}, f32[1,1,2048,384]{2,3,1,0:T(8,128)}, f32[1,1,2048,384]{2,3,1,0:T(8,128)}) conditional(s32[]{:T(128)} %clamp.3, (bf16[1,1,2048,384]{2,3,1,0:T(8,128)(2,1)S(1)}, bf16[1,1,128,2048]{3,2,1,0:T(8,128)(2,1)}, ...), branch_computations={%region_13.14_spmd, %region_14.15_spmd, %region_15.16_spmd} | conditional | flops 524288 | bytes 35651776
  235.8 2.6 collective-permute-start.7
  238.5 75.4 %collective-permute-done.5 = bf16[1,1,128,2048]{3,2,1,0:T(8,128)(2,1)S(1)} collective-permute-done((bf16[1,1,128,2048]{3,2,1,0:T(8,128)(2,1)}, bf16[1,1,128,2048]{3,2,1,0:T(8,128)(2,1)S(1)}, u32[]{:S(2)}, u32[]{:S(2)}) %collective-permute-start.5) | collective-permute-done | bytes 524320 | tf_op jit(solution)/shard_map/cond/branch_1_fun/ppermute | solution.py:21
  315.1 10.1 %collective-permute-done.7 = bf16[1,1,128,2048]{3,2,1,0:T(8,128)(2,1)S(1)} collective-permute-done((bf16[1,1,128,2048]{3,2,1,0:T(8,128)(2,1)}, bf16[1,1,128,2048]{3,2,1,0:T(8,128)(2,1)S(1)}, u32[]{:S(2)}, u32[]{:S(2)}) %collective-permute-start.7) | collective-permute-done | bytes 524320 | tf_op jit(solution)/shard_map/cond/branch_1_fun/ppermute | solution.py:21
  326.2 3.1 copy.33
  329.3 3.1 copy.36
  332.4 2.3 fusion.38
  334.7 3.5 fusion.6
  338.2 2.7 copy.27
  341.8 2.4 multiply_convert_fusion.1
  (79 shorter events, 38.2 us)
Async XLA Ops:
  7.2 172.6 %all-gather.2.cloned.1.call-start = ((), (), s32[]{:S(2)}) async-start(), calls=%async_computation.1 | async-start | bytes 8912896 | tf_op jit(solution)/shard_map/all_gather | solution.py:143
  15.8 140.0 %all-to-all-start = ((bf16[16,128,2048]{2,1,0:T(8,128)(2,1)}), bf16[16,128,2048]{2,1,0:T(8,128)(2,1)}, u32[]{:S(2)}, u32[]{:S(2)}) async-start(bf16[16,128,2048]{2,1,0:T(8,128)(2,1)} %stack.3), calls=%async_computation | async-start | bytes 16777216 | tf_op jit(solution)/shard_map/all_to_all | solution.py:158
  24.3 3.4 copy-start.3
  25.1 130.8 %copy-start.1 = (bf16[1,1,128,2048]{3,2,1,0:T(8,128)(2,1)S(1)}, bf16[1,1,128,2048]{3,2,1,0:T(8,128)(2,1)}, u32[]{:S(2)}) copy-start(bf16[1,1,128,2048]{3,2,1,0:T(8,128)(2,1)} %param.35) | copy-start | bytes 1572868
  155.9 23.9 %copy-start.4 = (bf16[1,1,2048,384]{3,2,1,0:T(8,128)(2,1)S(1)}, bf16[1,1,2048,384]{3,2,1,0:T(8,128)(2,1)}, u32[]{:S(2)}) copy-start(bf16[1,1,2048,384]{3,2,1,0:T(8,128)(2,1)} %param.34) | copy-start | bytes 4718596
  212.8 11.6 %slice-start = ((s8[8388608]{0:T(1024)(128)(4,1)}), s8[4194304]{0:T(1024)(128)(4,1)S(1)}, s32[]{:S(2)}) async-start(s8[8388608]{0:T(1024)(128)(4,1)} %bitcast.221), calls=%async_computation.2 | async-start | bytes 8388608
  217.2 1.1 copy-start.7
  217.2 7.2 %slice-start.1 = ((s8[8388608]{0:T(1024)(128)(4,1)}), s8[4194304]{0:T(1024)(128)(4,1)S(1)}, s32[]{:S(2)}) async-start(s8[8388608]{0:T(1024)(128)(4,1)} %bitcast.221), calls=%async_computation.3 | async-start | bytes 8388608
  218.3 6.1 %copy-start.5 = (bf16[1,1,2048,384]{2,3,1,0:T(8,128)(2,1)S(1)}, bf16[1,1,2048,384]{2,3,1,0:T(8,128)(2,1)}, u32[]{:S(2)}) copy-start(bf16[1,1,2048,384]{2,3,1,0:T(8,128)(2,1)} %copy.12) | copy-start | bytes 4718596
  218.3 6.1 %copy-start.6 = (bf16[1,1,2048,384]{2,3,1,0:T(8,128)(2,1)S(1)}, bf16[1,1,2048,384]{2,3,1,0:T(8,128)(2,1)}, u32[]{:S(2)}) copy-start(bf16[1,1,2048,384]{2,3,1,0:T(8,128)(2,1)} %copy.13) | copy-start | bytes 4718596
  229.9 96.3 %collective-permute-start.4 = (bf16[1,1,2048,384]{3,2,1,0:T(8,128)(2,1)}, bf16[1,1,2048,384]{3,2,1,0:T(8,128)(2,1)}, u32[]{:S(2)}, u32[]{:S(2)}) collective-permute-start(bf16[1,1,2048,384]{3,2,1,0:T(8,128)(2,1)} %copy.20), channel_id=1, source_target_pairs={{0,32},{16,48},{32,64},{48,80},{64,96},{80,112},{96,128},{112,144}... | collective-permute-start | bytes 4718600 | tf_op jit(solution)/shard_map/cond/branch_1_fun/ppermute | solution.py:21
  232.9 96.4 %collective-permute-start.6 = (bf16[1,1,2048,384]{3,2,1,0:T(8,128)(2,1)}, bf16[1,1,2048,384]{3,2,1,0:T(8,128)(2,1)}, u32[]{:S(2)}, u32[]{:S(2)}) collective-permute-start(bf16[1,1,2048,384]{3,2,1,0:T(8,128)(2,1)} %copy.21), channel_id=1, source_target_pairs={{0,32},{16,48},{32,64},{48,80},{64,96},{80,112},{96,128},{112,144}... | collective-permute-start | bytes 4718600 | tf_op jit(solution)/shard_map/cond/branch_1_fun/ppermute | solution.py:21
  234.4 79.5 %collective-permute-start.5 = (bf16[1,1,128,2048]{3,2,1,0:T(8,128)(2,1)}, bf16[1,1,128,2048]{3,2,1,0:T(8,128)(2,1)S(1)}, u32[]{:S(2)}, u32[]{:S(2)}) collective-permute-start(bf16[1,1,128,2048]{3,2,1,0:T(8,128)(2,1)} %get-tuple-element.165), channel_id=1, source_target_pairs={{0,32},{16,48},{32,64},{48,80},{64,96},{80,112},{96,128},{112,144}... | collective-permute-start | bytes 1572872 | tf_op jit(solution)/shard_map/cond/branch_1_fun/ppermute | solution.py:21
  235.8 89.3 %collective-permute-start.7 = (bf16[1,1,128,2048]{3,2,1,0:T(8,128)(2,1)}, bf16[1,1,128,2048]{3,2,1,0:T(8,128)(2,1)S(1)}, u32[]{:S(2)}, u32[]{:S(2)}) collective-permute-start(bf16[1,1,128,2048]{3,2,1,0:T(8,128)(2,1)} %get-tuple-element.167), channel_id=1, source_target_pairs={{0,32},{16,48},{32,64},{48,80},{64,96},{80,112},{96,128},{112,144}... | collective-permute-start | bytes 1572872 | tf_op jit(solution)/shard_map/cond/branch_1_fun/ppermute | solution.py:21
  338.2 2.7 copy-start
  338.2 2.7 copy-start.2
Sparse Core Ops, SparseCore 0:
  11.3 168.4 all-gather.1
